TPU v7x, 32 devices: a whole 2x2x4 slice. The times are simulated.
32 devices in a mesh: occ: 4 (over z), virt: 8 (over y, x, core).
Axes of the slice: x: 2, y: 2, z: 4, core: 2. Of those that a mesh axis runs over, the one named last changes fastest.
Arguments:
- amplitudes: float32 [128, 8192], P('occ', 'virt'), may hold values from -6 to 6
- tiles: float32 [2048, 128, 128], P(('occ', 'virt')), may hold values from -0.15625 to 0.15625
- tile_code: int32 [2048], P(('occ', 'virt')), may hold values from 0 to 127, as said below
- tile_count: int32 [32], P(('occ', 'virt')), may hold values from 16 to 64, as said below
- occ_energy: float32 [128], P('virt'), may hold values from -3 to -0.5
- virt_energy: float32 [8192], P('occ'), may hold values from 1 to 4
Outputs:
- updated: float32 [128, 8192], P('virt', 'occ')
Inputs may be any that keep to these rules, and one draw needn't show every extreme that they name: `tile_code`: within one device's 64 slots the positions are distinct. `tile_count`: some device has all 64 slots live.
All inputs are finite; a program needn't handle non-finite values.
Results may differ from a plain program's by a relative error of at most 0.0003.
Values sent between devices are 32-bit elements; how exact they have to be, the bound alone decides.
A program may use at most 64 MiB of HBM per device.

v0:
```python
import jax
import jax.numpy as jnp
from jax import lax
from jax.sharding import PartitionSpec as P


def contract(rows_block, tile_code, count, tiles, col_tiles):
    tile = tiles.shape[1]
    height = rows_block.shape[0]
    row_tiles = rows_block.shape[1] // tile
    blocked = rows_block.reshape(height, row_tiles, tile)
    groups = (count + 3) // 4

    def add_group(group, total):
        first = group * 4
        slot_ids = first + jnp.arange(4, dtype=jnp.int32)
        codes_now = lax.dynamic_slice_in_dim(tile_code, first, 4, 0)
        picked = lax.dynamic_slice_in_dim(tiles, first, 4, 0)
        live = (slot_ids < count).astype(jnp.float32)
        row_place = codes_now // col_tiles
        col_place = codes_now % col_tiles
        columns = jnp.take(blocked, row_place, axis=1)
        products = jnp.einsum("pgk,gkn->gpn", columns, picked, precision=lax.Precision.HIGHEST)
        products = products * live[:, None, None]
        for member in range(4):
            cstart = col_place[member] * tile
            present = lax.dynamic_slice_in_dim(total, cstart, tile, 1)
            total = lax.dynamic_update_slice_in_dim(total, present + products[member], cstart, 1)
        return total

    empty = jnp.zeros((height, col_tiles * tile), jnp.float32)
    return lax.fori_loop(0, groups, add_group, empty)


def body(amplitudes, tiles, tile_code, tile_count, occ_energy, virt_energy):
    count = tile_count[0]
    col_tiles = virt_energy.shape[0] // tiles.shape[1]
    partial_value = contract(
        lax.all_gather(amplitudes, "occ", axis=0, tiled=True), tile_code, count, tiles, col_tiles
    )
    mine = lax.psum_scatter(partial_value, "virt", scatter_dimension=0, tiled=True)
    return mine / (virt_energy[None, :] - occ_energy[:, None])


def solution(mesh):
    placed = (
        P("occ", "virt"),
        P(("occ", "virt"), None, None),
        P(("occ", "virt")),
        P(("occ", "virt")),
        P("virt"),
        P("occ"),
    )
    return jax.shard_map(
        body, mesh=mesh, in_specs=placed, out_specs=P("virt", "occ"), check_vma=False
    )
```

profile of v0, /device:TPU:0, one launch (start us, length us, event | category | flops | bytes accessed | tf_op | source)
XLA Modules:
  0.0 176.9 jit_solution(16554554797907972827)
XLA Ops:
  6.5 0.0 reduce-scatter.2.cloned.1.call-start
  7.2 17.6 %all_gather.3 = f32[128,1024]{1,0:T(8,128)S(1)} all-gather(f32[32,1024]{1,0:T(8,128)} %param.8), channel_id=1, replica_groups=mesh['occ'=4,'virt'=8] {'occ'}, dimensions={0}, use_global_device_ids=true | all-gather | bytes 655360 | tf_op jit(solution)/shard_map/all_gather | solution.py:39
  24.8 0.2 copy.10
  25.0 0.2 copy.11
  25.2 0.1 broadcast_in_dim.27
  25.3 0.0 copy-start.1
  25.3 0.0 copy-start.2
  25.3 53.5 %while.12 = (s32[]{:T(128)}, f32[128,2048]{1,0:T(8,128)S(1)}, s32[]{:T(128)}, s32[64]{0:T(128)}, f32[128,8,128]{2,0,1:T(8,128)S(1)}, /*index=5*/f32[64,128,128]{...) while((s32[]{:T(128)}, f32[128,2048]{1,0:T(8,128)S(1)}, ...), condition=%wide.region_1.2_spmd, body=%wide.region_0.1_spmd.sunk | while | flops 100861056 | bytes 2101819 | solution.py:32
  25.4 1.4 compare_and_fusion.2
  26.8 0.7 fusion.25
  30.0 0.6 gather_fusion
  30.5 1.4 convolution_multiply_fusion.2
  32.1 1.4 compare_and_fusion.2
  33.5 0.7 fusion.25
  36.7 0.6 gather_fusion
  37.2 1.4 convolution_multiply_fusion.2
  38.7 1.4 compare_and_fusion.2
  40.1 0.7 fusion.25
  43.3 0.6 gather_fusion
  43.9 1.4 convolution_multiply_fusion.2
  45.4 1.4 compare_and_fusion.2
  46.8 0.7 fusion.25
  50.0 0.6 gather_fusion
  50.6 1.4 convolution_multiply_fusion.2
  52.1 1.4 compare_and_fusion.2
  53.5 0.7 fusion.25
  56.7 0.6 gather_fusion
  57.3 1.4 convolution_multiply_fusion.2
  58.8 1.4 compare_and_fusion.2
  60.2 0.7 fusion.25
  63.4 0.6 gather_fusion
  64.0 1.4 convolution_multiply_fusion.2
  65.5 1.4 compare_and_fusion.2
  66.9 0.7 fusion.25
  70.1 0.6 gather_fusion
  70.7 1.4 convolution_multiply_fusion.2
  72.2 1.4 compare_and_fusion.2
  73.6 0.7 fusion.25
  76.8 0.6 gather_fusion
  77.4 1.4 convolution_multiply_fusion.2
  78.9 0.0 copy-start
  78.9 1.0 copy-done
  79.9 0.0 reduce-scatter.2.cloned.1.call-update
  79.9 88.5 %reduce-scatter.2.cloned.1.call-done = f32[16,2048]{1,0:T(8,128)} async-done(((f32[128,2048]{1,0:T(8,128)}), f32[16,2048]{1,0:T(8,128)}) %reduce-scatter.2.cloned.1.call-update) | async-done | bytes 131088 | tf_op jit(solution)/shard_map/reduce_scatter | solution.py:41
  168.4 0.0 copy-done.1
  168.4 0.0 copy-done.2
  168.4 1.7 subtract_divide_fusion
  (48 shorter events, 0.8 us)
Async XLA Ops:
  6.5 161.9 %reduce-scatter.2.cloned.1.call-start = ((), (), s32[]{:S(2)}) async-start(), calls=%async_computation.1 | async-start | bytes 1179648 | tf_op jit(solution)/shard_map/reduce_scatter | solution.py:41
  25.3 143.1 %copy-start.1 = (f32[2048]{0:T(1024)S(1)}, f32[2048]{0:T(1024)}, u32[]{:S(2)}) copy-start(f32[2048]{0:T(1024)} %param.13) | copy-start | bytes 24580
  25.3 143.1 %copy-start.2 = (f32[16]{0:T(128)S(1)}, f32[16]{0:T(128)}, u32[]{:S(2)}) copy-start(f32[16]{0:T(128)} %param.12) | copy-start | bytes 196
  78.9 1.0 copy-start
Sparse Core Ops, SparseCore 0:
  80.0 88.3 reduce-scatter.1
where the time goes:
time: 178 us; the launch traced here: 177 us
  waiting for transfers between devices  88.5 us (50%)
  loops' own time  20.8 us (12%)
  blocking collectives  17.6 us (10%)
  between operations  14.1 us (8%)
  other arithmetic  13.6 us (8%)
  local copies, waits for them, and re-layouts  11.2 us (6%)
  matrix products  11 us (6%)
    reduce_scatter x1, waiting for transfers between devices, body(): lax.psum_scatter(partial_value, 'virt', scatter_dimension=0, tiled=True)  88.5 us
    another operation x1, loops' own time, contract(): return lax.fori_loop(0, groups, add_group, empty)  20.8 us
    all_gather x1, blocking collectives, body(): lax.all_gather(amplitudes, 'occ', axis=0, tiled=True)  17.6 us
    and x8, other arithmetic, add_group(): columns = jnp.take(blocked, row_place, axis=1)  11.1 us
    dot_general x8, matrix products, add_group(): jnp.einsum('pgk,gkn->gpn', columns, picked, precision=lax.Precision.HIGHEST)  11 us
    slice x8, local copies, waits for them, and re-layouts, add_group(): cstart = col_place[member] * tile  5.26 us
    gather x8, local copies, waits for them, and re-layouts, add_group(): columns = jnp.take(blocked, row_place, axis=1)  4.52 us
  transfers between devices with their start and end apart: 1, of which 1 were waited for; matrix products, arithmetic and copies ran while one was open for 0% of the time, Pallas kernels for 0%

commit v1 on v0

v1 whole, which is shorter than its diff:
```python
import functools

import jax
import jax.numpy as jnp
from jax import lax
from jax.experimental import pallas as pl
from jax.experimental.pallas import tpu as pltpu
from jax.sharding import PartitionSpec as P

MESH = pl.DeviceIdType.MESH
SPLITS = 2
CHUNKS = 4


def flip(index, mask, size):
    out = index * 0
    bit = 1
    while bit < size:
        digit = lax.rem(lax.div(index, bit), 2)
        if mask & bit:
            digit = 1 - digit
        out = out + digit * bit
        bit *= 2
    return out


def kernel(
    no, nv,
    slot_ref, occ_ref, virt_ref, amp_in, tiles_in, out_ref,
    tiles, high, low, amp, lhs, part, partner_part, summed, arrived,
    tile_sem, own_sem, gather_send, gather_recv, core_send, core_recv, chip_send, chip_recv,
):
    o = lax.axis_index("occ")
    v = lax.axis_index("virt")
    core = lax.rem(v, 2)
    chip = lax.div(v, 2)
    chips = nv // 2
    block, depth = amp_in.shape
    tile = tiles_in.shape[1]
    width = out_ref.shape[1]
    rows = block * no
    dest = out_ref.shape[0]
    half = rows // 2
    col_tiles = width // tile
    positions = (depth // tile) * col_tiles
    slots = tiles_in.shape[0]

    tile_copy = pltpu.make_async_copy(tiles_in, tiles.at[pl.ds(0, slots)], tile_sem)
    tile_copy.start()
    own_copy = pltpu.make_async_copy(amp_in, amp.at[o], own_sem)
    own_copy.start()
    has_left = o > 0
    has_right = o < no - 1
    other_core = (o, v + 1 - 2 * core)

    barrier = pltpu.get_barrier_semaphore()

    @pl.when(has_left)
    def _():
        pl.semaphore_signal(barrier, inc=1, device_id=(o - 1, v), device_id_type=MESH)

    @pl.when(has_right)
    def _():
        pl.semaphore_signal(barrier, inc=1, device_id=(o + 1, v), device_id_type=MESH)

    pl.semaphore_signal(barrier, inc=1, device_id=other_core, device_id_type=MESH)
    for mask in range(1, chips):
        there = flip(chip, mask, chips)
        pl.semaphore_signal(barrier, inc=1, device_id=(o, 2 * there + core), device_id_type=MESH)
    tiles[slots] = jnp.zeros(tiles.shape[1:], tiles.dtype)
    pl.semaphore_wait(barrier, chips + has_left.astype(jnp.int32) + has_right.astype(jnp.int32))

    piece = block // SPLITS

    def gather_copy(source, which, split, side):
        return pltpu.make_async_remote_copy(
            src_ref=source,
            dst_ref=amp.at[which, pl.ds(split * piece, piece)],
            send_sem=gather_send.at[side, which, split],
            recv_sem=gather_recv.at[which, split],
            device_id=(o + 2 * side - 1, v),
            device_id_type=MESH,
        )

    def held(which, split):
        return amp.at[which, pl.ds(split * piece, piece)]

    for split in range(SPLITS):
        mine = amp_in.at[pl.ds(split * piece, piece)]

        @pl.when(has_right)
        def _():
            gather_copy(mine, o, split, 1).start()

        @pl.when(has_left)
        def _():
            gather_copy(mine, o, split, 0).start()

    def place(position, carry):
        value = tiles[slot_ref[position]]
        rounded = value.astype(jnp.bfloat16)
        at_row = pl.multiple_of(lax.div(position, col_tiles) * tile, tile)
        at_col = pl.multiple_of(lax.rem(position, col_tiles) * tile, tile)
        high[pl.ds(at_row, tile), pl.ds(at_col, tile)] = rounded
        low[pl.ds(at_row, tile), pl.ds(at_col, tile)] = (
            value - rounded.astype(jnp.float32)
        ).astype(jnp.bfloat16)
        return carry

    tile_copy.wait()
    steps = (no - 1) * SPLITS
    step = 0
    for distance in range(1, no):
        for split in range(SPLITS):
            lax.fori_loop(
                positions * step // steps, positions * (step + 1) // steps, place, 0
            )
            step += 1

            @pl.when(o >= distance)
            def _():
                which = o - distance
                gather_copy(held(which, split), which, split, 1).wait_recv()

                @pl.when(has_right)
                def _():
                    gather_copy(held(which, split), which, split, 1).start()

            @pl.when(o + distance < no)
            def _():
                which = o + distance
                gather_copy(held(which, split), which, split, 0).wait_recv()

                @pl.when(has_left)
                def _():
                    gather_copy(held(which, split), which, split, 0).start()

    own_copy.wait()
    groups = block // dest
    for which in range(no):
        for group in range(groups):
            target = which * groups + group
            start = (target % 2) * half + (target // 2) * dest
            value = amp[which, pl.ds(group * dest, dest)]
            rounded = value.astype(jnp.bfloat16)
            lhs[pl.ds(start, dest)] = rounded
            lhs[pl.ds(rows + start, dest)] = (
                value - rounded.astype(jnp.float32)
            ).astype(jnp.bfloat16)

    chunk = width // CHUNKS

    def core_copy(at):
        cols = pl.ds(at * chunk, chunk)
        return pltpu.make_async_remote_copy(
            src_ref=part.at[1 - core, :, cols],
            dst_ref=partner_part.at[:, cols],
            send_sem=core_send.at[at],
            recv_sem=core_recv.at[at],
            device_id=other_core,
            device_id_type=MESH,
        )

    def chip_copy(mask, at):
        cols = pl.ds(at * chunk, chunk)
        there = flip(chip, mask, chips)
        return pltpu.make_async_remote_copy(
            src_ref=summed.at[there, :, cols],
            dst_ref=arrived.at[mask - 1, :, cols],
            send_sem=chip_send.at[mask - 1, at],
            recv_sem=chip_recv.at[mask - 1, at],
            device_id=(o, 2 * there + core),
            device_id_type=MESH,
        )

    def pass_on(at):
        cols = pl.ds(at * chunk, chunk)
        core_copy(at).wait_recv()
        total = part[core, :, cols] + partner_part[:, cols]
        summed[:, :, cols] = total.reshape(chips, dest, chunk)
        for mask in range(chips - 1, 0, -1):
            chip_copy(mask, at).start()

    for at in range(CHUNKS):
        cols = pl.ds(at * chunk, chunk)
        wide = jnp.dot(lhs[...], high[:, cols], preferred_element_type=jnp.float32)
        narrow = jnp.dot(lhs[pl.ds(0, rows)], low[:, cols], preferred_element_type=jnp.float32)
        total = wide[:rows] + (wide[rows:] + narrow)
        part[:, :, cols] = total.reshape(2, half, chunk)
        core_copy(at).start()
        if at:
            pass_on(at - 1)
    pass_on(CHUNKS - 1)

    row_index = lax.broadcasted_iota(jnp.int32, (dest, chunk), 0)
    energy = jnp.zeros((dest, chunk), jnp.float32)
    for row in range(dest):
        energy = jnp.where(row_index == row, occ_ref[row], energy)
    for at in range(CHUNKS):
        cols = pl.ds(at * chunk, chunk)
        total = summed[chip, :, cols]
        for mask in range(1, chips):
            chip_copy(mask, at).wait_recv()
            total = total + arrived[mask - 1, :, cols]
        out_ref[:, cols] = total / (virt_ref[:, cols] - energy)

    for at in range(CHUNKS):
        core_copy(at).wait_send()
        for mask in range(1, chips):
            chip_copy(mask, at).wait_send()
    for which in range(no):
        for split in range(SPLITS):

            @pl.when(has_right & (o >= which))
            def _():
                gather_copy(held(which, split), which, split, 1).wait_send()

            @pl.when(has_left & (o <= which))
            def _():
                gather_copy(held(which, split), which, split, 0).wait_send()


def body(no, nv, amplitudes, tiles, tile_code, tile_count, occ_energy, virt_energy):
    block, depth = amplitudes.shape
    slots, tile, _ = tiles.shape
    width = virt_energy.shape[0]
    dest = occ_energy.shape[0]
    rows = block * no
    chips = nv // 2
    positions = (depth // tile) * (width // tile)
    grid = (slots, positions)
    slot_ids = lax.broadcasted_iota(jnp.int32, grid, 0)
    places = lax.broadcasted_iota(jnp.int32, grid, 1)
    hit = (tile_code[:, None] == places) & (slot_ids < tile_count[:, None])
    slot_of = jnp.min(jnp.where(hit, slot_ids, slots), axis=0)
    smem = pl.BlockSpec(memory_space=pltpu.SMEM)
    vmem = pl.BlockSpec(memory_space=pltpu.VMEM)
    anywhere = pl.BlockSpec(memory_space=pl.ANY)
    return pl.pallas_call(
        functools.partial(kernel, no, nv),
        out_shape=jax.ShapeDtypeStruct((dest, width), jnp.float32),
        in_specs=[smem, smem, vmem, anywhere, anywhere],
        out_specs=vmem,
        scratch_shapes=[
            pltpu.VMEM((slots + 1, tile, tile), jnp.float32),
            pltpu.VMEM((depth, width), jnp.bfloat16),
            pltpu.VMEM((depth, width), jnp.bfloat16),
            pltpu.VMEM((no, block, depth), jnp.float32),
            pltpu.VMEM((2 * rows, depth), jnp.bfloat16),
            pltpu.VMEM((2, rows // 2, width), jnp.float32),
            pltpu.VMEM((rows // 2, width), jnp.float32),
            pltpu.VMEM((chips, dest, width), jnp.float32),
            pltpu.VMEM((chips - 1, dest, width), jnp.float32),
            pltpu.SemaphoreType.DMA,
            pltpu.SemaphoreType.DMA,
            pltpu.SemaphoreType.DMA((2, no, SPLITS)),
            pltpu.SemaphoreType.DMA((no, SPLITS)),
            pltpu.SemaphoreType.DMA((CHUNKS,)),
            pltpu.SemaphoreType.DMA((CHUNKS,)),
            pltpu.SemaphoreType.DMA((chips - 1, CHUNKS)),
            pltpu.SemaphoreType.DMA((chips - 1, CHUNKS)),
        ],
        compiler_params=pltpu.CompilerParams(collective_id=0, has_side_effects=True),
    )(slot_of, occ_energy, virt_energy.reshape(1, width), amplitudes, tiles)


def solution(mesh):
    placed = (
        P("occ", "virt"),
        P(("occ", "virt"), None, None),
        P(("occ", "virt")),
        P(("occ", "virt")),
        P("virt"),
        P("occ"),
    )
    return jax.shard_map(
        functools.partial(body, mesh.shape["occ"], mesh.shape["virt"]),
        mesh=mesh, in_specs=placed, out_specs=P("virt", "occ"), check_vma=False,
    )
```

time: 178 us -> 31 us (0.17)
  waiting for transfers between devices: 88.5 us -> 0 us
  Pallas kernels: 0 us -> 27.3 us
  loops' own time: 20.8 us -> 0 us
  blocking collectives: 17.6 us -> 0 us
  between operations: 14.1 us -> 0.67 us
  other arithmetic: 13.6 us -> 1.27 us
  matrix products: 11 us -> 0 us
  local copies, waits for them, and re-layouts: 11.2 us -> 1.57 us
    reduce_scatter x1 -> x0, waiting for transfers between devices: 88.5 us -> none  [body(): lax.psum_scatter(partial_value, 'virt', scatter_dimension=0, tiled=True)]
    pallas_call x0 -> x1, Pallas kernels: none -> 27.3 us  [body(): pl.pallas_call(functools.partial(kernel, no, nv), out_shape=jax.ShapeDtyp...]
    another operation x1 -> x0, loops' own time: 20.8 us -> none  [contract(): return lax.fori_loop(0, groups, add_group, empty)]
    all_gather x1 -> x0, blocking collectives: 17.6 us -> none  [body(): lax.all_gather(amplitudes, 'occ', axis=0, tiled=True)]
    and x8 -> x0, other arithmetic: 11.1 us -> none  [add_group(): columns = jnp.take(blocked, row_place, axis=1)]
    dot_general x8 -> x0, matrix products: 11 us -> none  [add_group(): jnp.einsum('pgk,gkn->gpn', columns, picked, precision=lax.Precision.HIGHEST)]
    slice x8 -> x0, local copies, waits for them, and re-layouts: 5.26 us -> none  [add_group(): cstart = col_place[member] * tile]
    gather x8 -> x0, local copies, waits for them, and re-layouts: 4.52 us -> none  [add_group(): columns = jnp.take(blocked, row_place, axis=1)]
  transfers between devices with their start and end apart: 1 -> 0, of which waited for: 1 -> 0; matrix products, arithmetic and copies ran while one was open for 0% -> 0% of each run, Pallas kernels for 0% -> 0%
where the time goes in v1:
time: 31 us; the launch traced here: 30.8 us
  Pallas kernels  27.3 us (88%)
  local copies, waits for them, and re-layouts  1.57 us (5%)
  other arithmetic  1.27 us (4%)
  between operations  0.67 us (2%)
    pallas_call x1, Pallas kernels, body(): pl.pallas_call(functools.partial(kernel, no, nv), out_shape=jax.ShapeDtyp...  27.3 us
    unnamed x1, local copies, waits for them, and re-layouts  1.57 us
    reduce_min x1, other arithmetic, body(): slot_of = jnp.min(jnp.where(hit, slot_ids, slots), axis=0)  1.27 us

profile of v1, /device:TPU:0, one launch (start us, length us, event | category | flops | bytes accessed | tf_op | source)
XLA Modules:
  0.0 30.8 jit_solution(2976491656975706036)
XLA Ops:
  0.7 1.3 %select_reduce_fusion.slot_ref = s32[128]{0:T(128)} fusion(s32[64]{0:T(128)} %param.8, pred[64]{0:T(512)(128)(4,1)S(1)} %iota_compare_fusion.1), kind=kLoop, calls=%fused_computation | loop fusion | flops 32640 | bytes 832 | tf_op jit(solution)/shard_map/reduce_min | solution.py:235
  1.9 27.3 %shard_map.64 = f32[16,2048]{1,0:T(8,128)} custom-call(s32[128]{0:T(128)} %select_reduce_fusion.slot_ref, f32[16]{0:T(128)} %occ_ref.1, f32[1,2048]{1,0:T(1,128)} %bitcast.3, f32[32,1024]{1,0:T(8,128)} %amp_in.1, f32[64,128,128]{2,1,0:T(8,128)} %tiles_in.1), custom_call_target="tpu_custom_call" | custom-call | tf_op jit(solution)/shard_map/pallas_call | solution.py:239
  29.3 1.6 %copy.9 = f32[16,2048]{1,0:T(8,128)} copy(f32[16,2048]{1,0:T(8,128)} %shard_map.64) | data formatting | bytes 262144
  (1 shorter events, 0.0 us)

commit v2 on v1

v2 whole, which is shorter than its diff:
```python
import functools

import jax
import jax.numpy as jnp
from jax import lax
from jax.experimental import pallas as pl
from jax.experimental.pallas import tpu as pltpu
from jax.sharding import PartitionSpec as P

MESH = pl.DeviceIdType.MESH
PHASES = 2
CHUNKS = 4
GRANT = 50 * 2**20


def flip(index, mask, size):
    out = index * 0
    bit = 1
    while bit < size:
        digit = lax.rem(lax.div(index, bit), 2)
        if mask & bit:
            digit = 1 - digit
        out = out + digit * bit
        bit *= 2
    return out


def kernel(
    no, nv,
    code_in, count_in, occ_in, virt_in, amp_in, tiles_in, out_ref,
    code, count, occ_energy, virt_energy, slot_map, slot_of,
    tiles, high, low, amp, lhs, part, partner_part, summed, arrived,
    small_sem, slot_sem, tile_sem, own_sem,
    gather_send, gather_recv, core_send, core_recv, chip_send, chip_recv,
):
    o = lax.axis_index("occ")
    v = lax.axis_index("virt")
    core = lax.rem(v, 2)
    chip = lax.div(v, 2)
    chips = nv // 2
    depth = amp_in.shape[-1]
    tile = tiles_in.shape[1]
    dest, width = out_ref.shape
    level = dest // PHASES
    rows = lhs.shape[1] // 2
    half = rows // 2
    col_tiles = width // tile
    positions = (depth // tile) * col_tiles
    slots = tiles_in.shape[0]

    small = [
        pltpu.make_async_copy(source, target, small_sem.at[number])
        for number, (source, target) in enumerate(
            ((code_in, code), (count_in, count), (occ_in, occ_energy), (virt_in, virt_energy))
        )
    ]
    small[0].start()
    small[1].start()
    own_copy = pltpu.make_async_copy(amp_in, amp.at[o], own_sem)
    own_copy.start()
    tile_copy = pltpu.make_async_copy(tiles_in, tiles.at[pl.ds(0, slots)], tile_sem)
    tile_copy.start()
    small[2].start()
    small[3].start()
    has_left = o > 0
    has_right = o < no - 1
    other_core = (o, v + 1 - 2 * core)

    barrier = pltpu.get_barrier_semaphore()

    @pl.when(has_left)
    def _():
        pl.semaphore_signal(barrier, inc=1, device_id=(o - 1, v), device_id_type=MESH)

    @pl.when(has_right)
    def _():
        pl.semaphore_signal(barrier, inc=1, device_id=(o + 1, v), device_id_type=MESH)

    for mask in range(chips - 1, 0, -1):
        there = flip(chip, mask, chips)
        pl.semaphore_signal(barrier, inc=1, device_id=(o, 2 * there + core), device_id_type=MESH)
    pl.semaphore_signal(barrier, inc=1, device_id=other_core, device_id_type=MESH)

    tiles[slots] = jnp.zeros(tiles.shape[1:], tiles.dtype)
    small[0].wait()
    small[1].wait()
    lanes = slot_map.shape[1]
    place_index = lax.broadcasted_iota(jnp.int32, slot_map.shape, 0) * lanes + (
        lax.broadcasted_iota(jnp.int32, slot_map.shape, 1)
    )
    found = jnp.full(slot_map.shape, slots, jnp.int32)
    live = count[0]
    for slot in range(slots):
        found = jnp.where(place_index == jnp.where(slot < live, code[slot], -1), slot, found)
    slot_map[...] = found

    pl.semaphore_wait(barrier, chips + has_left.astype(jnp.int32) + has_right.astype(jnp.int32))

    def gather_copy(source, which, phase, side):
        return pltpu.make_async_remote_copy(
            src_ref=source,
            dst_ref=amp.at[which, :, :, phase],
            send_sem=gather_send.at[side, which, phase],
            recv_sem=gather_recv.at[which, phase],
            device_id=(o + 2 * side - 1, v),
            device_id_type=MESH,
        )

    def held(which, phase):
        return amp.at[which, :, :, phase]

    for phase in range(PHASES):
        mine = amp_in.at[:, :, phase]

        @pl.when(has_right)
        def _():
            gather_copy(mine, o, phase, 1).start()

        @pl.when(has_left)
        def _():
            gather_copy(mine, o, phase, 0).start()

    slot_copy = pltpu.make_async_copy(slot_map, slot_of, slot_sem)
    slot_copy.start()

    def place(position, carry):
        value = tiles[slot_of[lax.div(position, lanes), lax.rem(position, lanes)]]
        rounded = value.astype(jnp.bfloat16)
        at_row = pl.multiple_of(lax.div(position, col_tiles) * tile, tile)
        at_col = pl.multiple_of(lax.rem(position, col_tiles) * tile, tile)
        high[pl.ds(at_row, tile), pl.ds(at_col, tile)] = rounded
        low[pl.ds(at_row, tile), pl.ds(at_col, tile)] = (
            value - rounded.astype(jnp.float32)
        ).astype(jnp.bfloat16)
        return carry

    def relay(phase, distance):
        @pl.when(o >= distance)
        def _():
            which = o - distance
            gather_copy(held(which, phase), which, phase, 1).wait_recv()

            @pl.when(has_right)
            def _():
                gather_copy(held(which, phase), which, phase, 1).start()

        @pl.when(o + distance < no)
        def _():
            which = o + distance
            gather_copy(held(which, phase), which, phase, 0).wait_recv()

            @pl.when(has_left)
            def _():
                gather_copy(held(which, phase), which, phase, 0).start()

    chunk = width // CHUNKS

    def split(phase):
        for side in range(2):
            value = amp[:, :, side, phase].reshape(half, depth)
            rounded = value.astype(jnp.bfloat16)
            lhs[phase, pl.ds(side * half, half)] = rounded
            lhs[phase, pl.ds(rows + side * half, half)] = (
                value - rounded.astype(jnp.float32)
            ).astype(jnp.bfloat16)

    def core_copy(phase, at):
        cols = pl.ds(at * chunk, chunk)
        return pltpu.make_async_remote_copy(
            src_ref=part.at[phase, 1 - core, :, cols],
            dst_ref=partner_part.at[phase, :, cols],
            send_sem=core_send.at[phase, at],
            recv_sem=core_recv.at[phase, at],
            device_id=other_core,
            device_id_type=MESH,
        )

    def chip_copy(phase, mask, at):
        cols = pl.ds(at * chunk, chunk)
        there = flip(chip, mask, chips)
        return pltpu.make_async_remote_copy(
            src_ref=summed.at[phase, there, :, cols],
            dst_ref=arrived.at[phase, mask - 1, :, cols],
            send_sem=chip_send.at[phase, mask - 1, at],
            recv_sem=chip_recv.at[phase, mask - 1, at],
            device_id=(o, 2 * there + core),
            device_id_type=MESH,
        )

    def multiply(phase, at):
        cols = pl.ds(at * chunk, chunk)
        wide = jnp.dot(lhs[phase], high[:, cols], preferred_element_type=jnp.float32)
        narrow = jnp.dot(
            lhs[phase, pl.ds(0, rows)], low[:, cols], preferred_element_type=jnp.float32
        )
        total = wide[:rows] + (wide[rows:] + narrow)
        part[phase, :, :, cols] = total.reshape(2, half, chunk)
        core_copy(phase, at).start()

    def pass_on(phase, at):
        cols = pl.ds(at * chunk, chunk)
        core_copy(phase, at).wait_recv()
        total = part[phase, core, :, cols] + partner_part[phase, :, cols]
        summed[phase, :, :, cols] = total.reshape(chips, level, chunk)
        for mask in range(chips - 1, 0, -1):
            chip_copy(phase, mask, at).start()

    def job(phase, at):
        if at == 0:
            split(phase)
        if at < CHUNKS:
            multiply(phase, at)
        if at:
            pass_on(phase, at - 1)

    tile_copy.wait()
    slot_copy.wait()
    for phase in range(PHASES):
        for distance in range(1, no):
            if phase == 0:
                lax.fori_loop(
                    positions * (distance - 1) // (no - 1),
                    positions * distance // (no - 1),
                    place,
                    0,
                )
            elif distance > 1:
                for at in range(
                    (CHUNKS + 1) * (distance - 2) // (no - 2), (CHUNKS + 1) * (distance - 1) // (no - 2)
                ):
                    job(phase - 1, at)
            relay(phase, distance)
        if phase == 0:
            own_copy.wait()
        elif no == 2:
            for at in range(CHUNKS + 1):
                job(phase - 1, at)
    for at in range(CHUNKS + 1):
        job(PHASES - 1, at)

    small[2].wait()
    small[3].wait()
    shape = (level, chunk)
    row_index = lax.broadcasted_iota(jnp.int32, shape, 0)
    for phase in range(PHASES):
        energy = jnp.zeros(shape, jnp.float32)
        for row in range(level):
            energy = jnp.where(row_index == row, occ_energy[phase * level + row], energy)
        for at in range(CHUNKS):
            cols = pl.ds(at * chunk, chunk)
            total = summed[phase, chip, :, cols]
            for mask in range(1, chips):
                chip_copy(phase, mask, at).wait_recv()
                total = total + arrived[phase, mask - 1, :, cols]
            out_ref[pl.ds(phase * level, level), cols] = total / (virt_energy[:, cols] - energy)

    for phase in range(PHASES):
        for at in range(CHUNKS):
            core_copy(phase, at).wait_send()
            for mask in range(1, chips):
                chip_copy(phase, mask, at).wait_send()
        for which in range(no):

            @pl.when(has_right & (o >= which))
            def _():
                gather_copy(held(which, phase), which, phase, 1).wait_send()

            @pl.when(has_left & (o <= which))
            def _():
                gather_copy(held(which, phase), which, phase, 0).wait_send()


def body(no, nv, amplitudes, tiles, tile_code, tile_count, occ_energy, virt_energy):
    block, depth = amplitudes.shape
    slots, tile, _ = tiles.shape
    width = virt_energy.shape[0]
    dest = occ_energy.shape[0]
    chips = nv // 2
    level = dest // PHASES
    pairs = block // (2 * dest)
    rows = block * no // PHASES
    map_shape = (max(8, (depth // tile) * (width // tile) // 128), 128)
    f32, bf16, i32 = jnp.float32, jnp.bfloat16, jnp.int32
    vmem, smem, dma = pltpu.VMEM, pltpu.SMEM, pltpu.SemaphoreType.DMA
    return pl.pallas_call(
        functools.partial(kernel, no, nv),
        out_shape=jax.ShapeDtypeStruct((dest, width), f32),
        in_specs=[pl.BlockSpec(memory_space=pltpu.HBM)] * 6,
        out_specs=pl.BlockSpec(memory_space=pltpu.VMEM),
        scratch_shapes=[
            smem(tile_code.shape, i32),
            smem(tile_count.shape, i32),
            smem((dest,), f32),
            vmem((1, width), f32),
            vmem(map_shape, i32),
            smem(map_shape, i32),
            vmem((slots + 1, tile, tile), f32),
            vmem((depth, width), bf16),
            vmem((depth, width), bf16),
            vmem((no, pairs, 2, PHASES, level, depth), f32),
            vmem((PHASES, 2 * rows, depth), bf16),
            vmem((PHASES, 2, rows // 2, width), f32),
            vmem((PHASES, rows // 2, width), f32),
            vmem((PHASES, chips, level, width), f32),
            vmem((PHASES, chips - 1, level, width), f32),
            dma((4,)),
            dma,
            dma,
            dma,
            dma((2, no, PHASES)),
            dma((no, PHASES)),
            dma((PHASES, CHUNKS)),
            dma((PHASES, CHUNKS)),
            dma((PHASES, chips - 1, CHUNKS)),
            dma((PHASES, chips - 1, CHUNKS)),
        ],
        compiler_params=pltpu.CompilerParams(
            collective_id=0, has_side_effects=True, vmem_limit_bytes=GRANT
        ),
    )(
        tile_code,
        tile_count,
        occ_energy,
        virt_energy.reshape(1, width),
        amplitudes.reshape(pairs, 2, PHASES, level, depth),
        tiles,
    )


def solution(mesh):
    placed = (
        P("occ", "virt"),
        P(("occ", "virt"), None, None),
        P(("occ", "virt")),
        P(("occ", "virt")),
        P("virt"),
        P("occ"),
    )
    return jax.shard_map(
        functools.partial(body, mesh.shape["occ"], mesh.shape["virt"]),
        mesh=mesh, in_specs=placed, out_specs=P("virt", "occ"), check_vma=False,
    )
```

time: 31 us -> 30.7 us (level)
  local copies, waits for them, and re-layouts: 1.57 us -> 3.56 us
  other arithmetic: 1.27 us -> 0 us
  Pallas kernels: 27.3 us -> 26.3 us
    unnamed x1 -> x9, local copies, waits for them, and re-layouts: 1.57 us -> 3.56 us
    reduce_min x1 -> x0, other arithmetic: 1.27 us -> none  [body(): slot_of = jnp.min(jnp.where(hit, slot_ids, slots), axis=0)]
    pallas_call x1, Pallas kernels: 27.3 us -> 26.3 us  [body(): pl.pallas_call(functools.partial(kernel, no, nv), out_shape=jax.ShapeDtyp...]
where the time goes in v2:
time: 30.7 us; the launch traced here: 30.5 us
  Pallas kernels  26.3 us (86%)
  local copies, waits for them, and re-layouts  3.56 us (12%)
  between operations  0.67 us (2%)
    pallas_call x1, Pallas kernels, body(): pl.pallas_call(functools.partial(kernel, no, nv), out_shape=jax.ShapeDtyp...  26.3 us
    unnamed x9, local copies, waits for them, and re-layouts  3.56 us

profile of v2, /device:TPU:0, one launch (start us, length us, event | category | flops | bytes accessed | tf_op | source)
XLA Modules:
  0.0 30.5 jit_solution(8202790824216809699)
XLA Ops:
  0.7 0.0 copy-start
  0.7 0.9 %copy-done = f32[32,1024]{1,0:T(8,128)S(1)} copy-done((f32[32,1024]{1,0:T(8,128)S(1)}, f32[32,1024]{1,0:T(8,128)}, u32[]{:S(2)}) %copy-start) | copy-done | bytes 131096
  1.6 0.0 copy-start.1
  1.6 0.7 %copy-done.1 = f32[2048]{0:T(1024)S(1)} copy-done((f32[2048]{0:T(1024)S(1)}, f32[2048]{0:T(1024)}, u32[]{:S(2)}) %copy-start.1) | copy-done | bytes 8216
  2.3 0.0 copy-start.2
  2.3 0.7 %copy-done.2 = s32[64]{0:T(128)S(1)} copy-done((s32[64]{0:T(128)S(1)}, s32[64]{0:T(128)}, u32[]{:S(2)}) %copy-start.2) | copy-done | bytes 280
  2.9 0.0 copy-start.3
  2.9 0.7 %copy-done.3 = f32[16]{0:T(128)S(1)} copy-done((f32[16]{0:T(128)S(1)}, f32[16]{0:T(128)}, u32[]{:S(2)}) %copy-start.3) | copy-done | bytes 88
  3.6 26.3 %shard_map.64 = f32[16,2048]{1,0:T(8,128)S(1)} custom-call(s32[64]{0:T(128)S(1)} %copy-done.2, s32[1]{0:T(128)S(6)} %copy.8.count_in, f32[16]{0:T(128)S(1)} %copy-done.3, f32[1,2048]{1,0:T(1,128)S(1)} %bitcast.3, f32[1,2,2,8,1024]{4,3,2,1,0:T(8,128)S(1)} %bitcast.2, f32[64,128,128]{2,1,0:T(8,128)} %tiles_in.1), custom_call_target="tpu_custom_call" | custom-call | tf_op jit(solution)/shard_map/pallas_call | solution.py:285
  29.9 0.7 %copy.9 = f32[16,2048]{1,0:T(8,128)} copy(f32[16,2048]{1,0:T(8,128)S(1)} %shard_map.64) | data formatting | bytes 262144
Async XLA Ops:
  0.7 0.9 %copy-start = (f32[32,1024]{1,0:T(8,128)S(1)}, f32[32,1024]{1,0:T(8,128)}, u32[]{:S(2)}) copy-start(f32[32,1024]{1,0:T(8,128)} %param.6) | copy-start | bytes 393220
  1.6 0.7 %copy-start.1 = (f32[2048]{0:T(1024)S(1)}, f32[2048]{0:T(1024)}, u32[]{:S(2)}) copy-start(f32[2048]{0:T(1024)} %param.11) | copy-start | bytes 24580
  2.3 0.7 %copy-start.2 = (s32[64]{0:T(128)S(1)}, s32[64]{0:T(128)}, u32[]{:S(2)}) copy-start(s32[64]{0:T(128)} %code_in.1) | copy-start | bytes 772
  2.9 0.7 %copy-start.3 = (f32[16]{0:T(128)S(1)}, f32[16]{0:T(128)}, u32[]{:S(2)}) copy-start(f32[16]{0:T(128)} %occ_in.1) | copy-start | bytes 196

commit v3 on v2

--- a/solution.py
+++ b/solution.py
@@ -210,8 +210,10 @@
             split(phase)
         if at < CHUNKS:
             multiply(phase, at)
-        if at:
-            pass_on(phase, at - 1)
+        else:
+            pass_on(phase, at - CHUNKS)
+
+    jobs = 2 * CHUNKS
 
     tile_copy.wait()
     slot_copy.wait()
@@ -226,16 +228,16 @@
                 )
             elif distance > 1:
                 for at in range(
-                    (CHUNKS + 1) * (distance - 2) // (no - 2), (CHUNKS + 1) * (distance - 1) // (no - 2)
+                    jobs * (distance - 2) // (no - 2), jobs * (distance - 1) // (no - 2)
                 ):
                     job(phase - 1, at)
             relay(phase, distance)
         if phase == 0:
             own_copy.wait()
         elif no == 2:
-            for at in range(CHUNKS + 1):
+            for at in range(jobs):
                 job(phase - 1, at)
-    for at in range(CHUNKS + 1):
+    for at in range(jobs):
         job(PHASES - 1, at)
 
     small[2].wait()
@@ -318,12 +320,17 @@
             collective_id=0, has_side_effects=True, vmem_limit_bytes=GRANT
         ),
     )(
-        tile_code,
-        tile_count,
-        occ_energy,
-        virt_energy.reshape(1, width),
-        amplitudes.reshape(pairs, 2, PHASES, level, depth),
-        tiles,
+        *(
+            a if a is tile_count else pltpu.with_memory_space_constraint(a, pltpu.HBM)
+            for a in (
+                tile_code,
+                tile_count,
+                occ_energy,
+                virt_energy.reshape(1, width),
+                amplitudes.reshape(pairs, 2, PHASES, level, depth),
+                tiles,
+            )
+        )
     )
 
 

time: 30.7 us -> 28.3 us (0.922)
  local copies, waits for them, and re-layouts: 3.56 us -> 0.66 us
  Pallas kernels: 26.3 us -> 26.8 us
    unnamed x9 -> x1, local copies, waits for them, and re-layouts: 3.56 us -> 0.66 us
    pallas_call x1, Pallas kernels: 26.3 us -> 26.8 us  [body(): pl.pallas_call(functools.partial(kernel, no, nv), out_shape=jax.ShapeDtyp...]
where the time goes in v3:
time: 28.3 us; the launch traced here: 28.1 us
  Pallas kernels  26.8 us (95%)
  local copies, waits for them, and re-layouts  0.66 us (2%)
  between operations  0.66 us (2%)
    pallas_call x1, Pallas kernels, body(): pl.pallas_call(functools.partial(kernel, no, nv), out_shape=jax.ShapeDtyp...  26.8 us
    unnamed x1, local copies, waits for them, and re-layouts  0.66 us

profile of v3, /device:TPU:0, one launch (start us, length us, event | category | flops | bytes accessed | tf_op | source)
XLA Modules:
  0.0 28.1 jit_solution(8083300218710813305)
XLA Ops:
  0.7 26.8 %shard_map.64 = f32[16,2048]{1,0:T(8,128)S(1)} custom-call(s32[64]{0:T(128)} %code_in.1, s32[1]{0:T(128)S(6)} %copy.8.count_in, f32[16]{0:T(128)} %occ_in.1, f32[1,2048]{1,0:T(1,128)} %bitcast.3, f32[1,2,2,8,1024]{4,3,2,1,0:T(8,128)} %bitcast.2, f32[64,128,128]{2,1,0:T(8,128)} %tiles_in.1), custom_call_target="tpu_custom_call" | custom-call | tf_op jit(solution)/shard_map/pallas_call | solution.py:287
  27.4 0.7 %copy.9 = f32[16,2048]{1,0:T(8,128)} copy(f32[16,2048]{1,0:T(8,128)S(1)} %shard_map.64) | data formatting | bytes 262144

commit v4 on v3

--- a/solution.py
+++ b/solution.py
@@ -205,40 +205,37 @@
         for mask in range(chips - 1, 0, -1):
             chip_copy(phase, mask, at).start()
 
-    def job(phase, at):
-        if at == 0:
-            split(phase)
-        if at < CHUNKS:
-            multiply(phase, at)
-        else:
-            pass_on(phase, at - CHUNKS)
-
-    jobs = 2 * CHUNKS
-
     tile_copy.wait()
     slot_copy.wait()
-    for phase in range(PHASES):
-        for distance in range(1, no):
-            if phase == 0:
-                lax.fori_loop(
-                    positions * (distance - 1) // (no - 1),
-                    positions * distance // (no - 1),
-                    place,
-                    0,
-                )
-            elif distance > 1:
-                for at in range(
-                    jobs * (distance - 2) // (no - 2), jobs * (distance - 1) // (no - 2)
-                ):
-                    job(phase - 1, at)
-            relay(phase, distance)
-        if phase == 0:
-            own_copy.wait()
-        elif no == 2:
-            for at in range(jobs):
-                job(phase - 1, at)
-    for at in range(jobs):
-        job(PHASES - 1, at)
+    own_copy.wait()
+    far = jnp.maximum(o, no - 1 - o)
+    parts = max(no // 2, 1)
+
+    def round_of(distance, carry):
+        first = lax.div(positions * (distance - 1), parts)
+        last = lax.div(positions * distance, parts)
+        lax.fori_loop(
+            jnp.minimum(first, positions), jnp.minimum(last, positions), place, 0
+        )
+        relay(0, distance)
+
+        @pl.when(distance == far)
+        def _():
+            split(0)
+            for at in range(CHUNKS):
+                multiply(0, at)
+
+        relay(1, distance)
+        return carry
+
+    lax.fori_loop(1, no, round_of, 0)
+    for at in range(CHUNKS):
+        pass_on(0, at)
+    split(1)
+    for at in range(CHUNKS):
+        multiply(1, at)
+    for at in range(CHUNKS):
+        pass_on(1, at)
 
     small[2].wait()
     small[3].wait()

time: 28.3 us -> 27.6 us (0.975)
  Pallas kernels: 26.8 us -> 26.1 us
    pallas_call x1, Pallas kernels: 26.8 us -> 26.1 us  [body(): pl.pallas_call(functools.partial(kernel, no, nv), out_shape=jax.ShapeDtyp...]
where the time goes in v4:
time: 27.6 us; the launch traced here: 27.4 us
  Pallas kernels  26.1 us (95%)
  local copies, waits for them, and re-layouts  0.66 us (2%)
  between operations  0.66 us (2%)
    pallas_call x1, Pallas kernels, body(): pl.pallas_call(functools.partial(kernel, no, nv), out_shape=jax.ShapeDtyp...  26.1 us
    unnamed x1, local copies, waits for them, and re-layouts  0.66 us

profile of v4, /device:TPU:0, one launch (start us, length us, event | category | flops | bytes accessed | tf_op | source)
XLA Modules:
  0.0 27.4 jit_solution(17627659679509743563)
XLA Ops:
  0.7 26.1 %shard_map.64 = f32[16,2048]{1,0:T(8,128)S(1)} custom-call(s32[64]{0:T(128)} %code_in.1, s32[1]{0:T(128)S(6)} %copy.8.count_in, f32[16]{0:T(128)} %occ_in.1, f32[1,2048]{1,0:T(1,128)} %bitcast.3, f32[1,2,2,8,1024]{4,3,2,1,0:T(8,128)} %bitcast.2, f32[64,128,128]{2,1,0:T(8,128)} %tiles_in.1), custom_call_target="tpu_custom_call" | custom-call | tf_op jit(solution)/shard_map/pallas_call | solution.py:284
  26.8 0.7 %copy.9 = f32[16,2048]{1,0:T(8,128)} copy(f32[16,2048]{1,0:T(8,128)S(1)} %shard_map.64) | data formatting | bytes 262144

commit v5 on v4

--- a/solution.py
+++ b/solution.py
@@ -81,7 +81,32 @@
         pl.semaphore_signal(barrier, inc=1, device_id=(o, 2 * there + core), device_id_type=MESH)
     pl.semaphore_signal(barrier, inc=1, device_id=other_core, device_id_type=MESH)
 
-    tiles[slots] = jnp.zeros(tiles.shape[1:], tiles.dtype)
+    pl.semaphore_wait(barrier, chips + has_left.astype(jnp.int32) + has_right.astype(jnp.int32))
+
+    def gather_copy(source, which, phase, side):
+        return pltpu.make_async_remote_copy(
+            src_ref=source,
+            dst_ref=amp.at[which, :, :, phase],
+            send_sem=gather_send.at[side, which, phase],
+            recv_sem=gather_recv.at[which, phase],
+            device_id=(o + 2 * side - 1, v),
+            device_id_type=MESH,
+        )
+
+    def held(which, phase):
+        return amp.at[which, :, :, phase]
+
+    for phase in range(PHASES):
+        mine = amp_in.at[:, :, phase]
+
+        @pl.when(has_right)
+        def _():
+            gather_copy(mine, o, phase, 1).start()
+
+        @pl.when(has_left)
+        def _():
+            gather_copy(mine, o, phase, 0).start()
+
     small[0].wait()
     small[1].wait()
     lanes = slot_map.shape[1]
@@ -93,33 +118,9 @@
     for slot in range(slots):
         found = jnp.where(place_index == jnp.where(slot < live, code[slot], -1), slot, found)
     slot_map[...] = found
-
-    pl.semaphore_wait(barrier, chips + has_left.astype(jnp.int32) + has_right.astype(jnp.int32))
-
-    def gather_copy(source, which, phase, side):
-        return pltpu.make_async_remote_copy(
-            src_ref=source,
-            dst_ref=amp.at[which, :, :, phase],
-            send_sem=gather_send.at[side, which, phase],
-            recv_sem=gather_recv.at[which, phase],
-            device_id=(o + 2 * side - 1, v),
-            device_id_type=MESH,
-        )
-
-    def held(which, phase):
-        return amp.at[which, :, :, phase]
-
-    for phase in range(PHASES):
-        mine = amp_in.at[:, :, phase]
-
-        @pl.when(has_right)
-        def _():
-            gather_copy(mine, o, phase, 1).start()
-
-        @pl.when(has_left)
-        def _():
-            gather_copy(mine, o, phase, 0).start()
-
+    own_copy.wait()
+    tile_copy.wait()
+    tiles[slots] = jnp.zeros(tiles.shape[1:], tiles.dtype)
     slot_copy = pltpu.make_async_copy(slot_map, slot_of, slot_sem)
     slot_copy.start()
 
@@ -205,9 +206,7 @@
         for mask in range(chips - 1, 0, -1):
             chip_copy(phase, mask, at).start()
 
-    tile_copy.wait()
     slot_copy.wait()
-    own_copy.wait()
     far = jnp.maximum(o, no - 1 - o)
     parts = max(no // 2, 1)
 

time: 27.6 us -> 27.7 us (level)
  no operation moved by 1% of the time
where the time goes in v5:
time: 27.7 us; the launch traced here: 27.5 us
  Pallas kernels  26.2 us (95%)
  local copies, waits for them, and re-layouts  0.66 us (2%)
  between operations  0.66 us (2%)
    pallas_call x1, Pallas kernels, body(): pl.pallas_call(functools.partial(kernel, no, nv), out_shape=jax.ShapeDtyp...  26.2 us
    unnamed x1, local copies, waits for them, and re-layouts  0.66 us

profile of v5, /device:TPU:0, one launch (start us, length us, event | category | flops | bytes accessed | tf_op | source)
XLA Modules:
  0.0 27.5 jit_solution(17502278465116381010)
XLA Ops:
  0.7 26.2 %shard_map.64 = f32[16,2048]{1,0:T(8,128)S(1)} custom-call(s32[64]{0:T(128)} %code_in.1, s32[1]{0:T(128)S(6)} %copy.8.count_in, f32[16]{0:T(128)} %occ_in.1, f32[1,2048]{1,0:T(1,128)} %bitcast.3, f32[1,2,2,8,1024]{4,3,2,1,0:T(8,128)} %bitcast.2, f32[64,128,128]{2,1,0:T(8,128)} %tiles_in.1), custom_call_target="tpu_custom_call" | custom-call | tf_op jit(solution)/shard_map/pallas_call | solution.py:283
  26.9 0.7 %copy.9 = f32[16,2048]{1,0:T(8,128)} copy(f32[16,2048]{1,0:T(8,128)S(1)} %shard_map.64) | data formatting | bytes 262144
